TPU v7x, 32 devices: a whole 2x2x4 slice. The times are simulated.
32 devices in a mesh: gy: 4 (over y, x), gx: 8 (over z, core).
Axes of the slice: x: 2, y: 2, z: 4, core: 2. Of those that a mesh axis runs over, the one named last changes fastest.
Arguments:
- cost_volume: int32 [64, 128, 256], P('gy', 'gx'), may hold values from 0 to 64
- left_image: float32 [64, 128], P('gy', 'gx'), may hold values from -6 to 6
- p_small: int32 [4], replicated, may hold values from 4 to 16
- p_large: int32 [4], replicated, may hold values from 32 to 128
Outputs:
- aggregated: float32 [64, 128, 256], P('gy', 'gx')
Inputs may be any that keep to these rules, and one draw needn't show every extreme that they name: `p_small`: every small penalty is below every large penalty.
All inputs are finite; a program needn't handle non-finite values.
Results may differ from a plain program's by a relative error of at most 0.00002.
Values sent between devices are 32-bit elements; how exact they have to be, the bound alone decides.
A program may use at most 64 MiB of HBM per device.

v0:
```python
from functools import partial

import jax
import jax.numpy as jnp
from jax import lax
from jax.sharding import PartitionSpec as P

FAR = 1e30
GRADIENT_GAIN = 4.0
OUT_SCALE = 1.0 / 256.0


def shifted(shard, axis, by):
    length = lax.axis_size(axis)
    pairs = [(i, i + by) for i in range(length) if 0 <= i + by < length]
    return lax.ppermute(shard, axis, pairs)


def padded_2(block, sides, width):
    for axis, dim in sides:
        count = lax.axis_size(axis)
        forward = [(i, i + 1) for i in range(count - 1)]
        backward = [(target, source) for source, target in forward]
        low = lax.ppermute(
            lax.slice_in_dim(block, block.shape[dim] - width, None, axis=dim), axis, forward
        )
        high = lax.ppermute(lax.slice_in_dim(block, 0, width, axis=dim), axis, backward)
        block = jnp.concatenate([low, block, high], axis=dim)
    return block


def advance(previous, inputs, penalty_one):
    cost_line, large_line = inputs
    lowest = jnp.min(previous, axis=-1, keepdims=True)
    padded = jnp.pad(previous, ((0, 0), (1, 1)), constant_values=FAR)
    neighbour = jnp.minimum(padded[:, :-2], padded[:, 2:]) + penalty_one
    chosen = jnp.minimum(jnp.minimum(previous, neighbour), lowest + large_line[:, None])
    updated = cost_line.astype(jnp.float32) + chosen - lowest
    return (updated, updated)


def sweep(cost_lines, large_lines, penalty_one, start, backward):
    boundary, path_part = lax.scan(
        partial(advance, penalty_one=penalty_one),
        start,
        (cost_lines, large_lines),
        reverse=backward,
    )
    return (path_part, boundary)


def adaptive(penalty_one, penalty_two, step_diff):
    return penalty_one + (penalty_two - penalty_one) / (1.0 + GRADIENT_GAIN * jnp.abs(step_diff))


def send_right(message):
    return shifted(message, "gx", 1)


def send_left(message):
    return shifted(message, "gx", -1)


def send_down(message):
    return shifted(message, "gy", 1)


def send_up(message):
    return shifted(message, "gy", -1)


def run_lane(
    step_index, running, incoming, cost_lines, large_lines, penalty_one, position, pieces, backward
):
    block_id = step_index - position
    active = jnp.logical_and(block_id >= 0, block_id < pieces)

    def process(running):
        path_part, boundary = sweep(cost_lines, large_lines, penalty_one, incoming, backward)
        return (running + path_part, boundary)

    def passing(running):
        return (running, jnp.zeros_like(incoming))

    return lax.cond(active, process, passing, running)


def on_device(cost_volume, left_image, p_small, p_large):
    tile_rows, tile_cols, disparities = cost_volume.shape
    pieces = 1
    padded = padded_2(left_image, (("gy", 0), ("gx", 1)), 1)
    middle = padded[1:-1, 1:-1]
    small_pens = p_small.astype(jnp.float32)
    large_pens = p_large.astype(jnp.float32)
    plain_right = adaptive(small_pens[0], large_pens[0], middle - padded[1:-1, :-2])
    plain_left = adaptive(small_pens[1], large_pens[1], middle - padded[1:-1, 2:])
    penalty_down = adaptive(small_pens[2], large_pens[2], middle - padded[:-2, 1:-1])
    penalty_up = adaptive(small_pens[3], large_pens[3], middle - padded[2:, 1:-1])
    count_x = lax.axis_size("gx")
    count_y = lax.axis_size("gy")
    penalty_right = plain_right.T
    penalty_left = plain_left.T
    crossed = jnp.transpose(cost_volume, (1, 0, 2))
    index_x = lax.axis_index("gx")
    index_y = lax.axis_index("gy")
    start_rows = jnp.zeros((tile_rows // pieces, disparities), jnp.float32)
    start_cols = jnp.zeros((tile_cols // pieces, disparities), jnp.float32)
    across = jnp.zeros((tile_cols, tile_rows, disparities), jnp.float32)
    down_total = jnp.zeros((tile_rows, tile_cols, disparities), jnp.float32)

    def horizontal(step_index, across, from_left, from_right):
        across, out_right = run_lane(
            step_index,
            across,
            from_left,
            crossed,
            penalty_right,
            small_pens[0],
            index_x,
            pieces,
            False,
        )
        across, out_left = run_lane(
            step_index,
            across,
            from_right,
            crossed,
            penalty_left,
            small_pens[1],
            count_x - 1 - index_x,
            pieces,
            True,
        )
        return (across, send_right(out_right), send_left(out_left))

    def vertical(step_index, down_total, from_above, from_below):
        down_total, out_down = run_lane(
            step_index,
            down_total,
            from_above,
            cost_volume,
            penalty_down,
            small_pens[2],
            index_y,
            pieces,
            False,
        )
        down_total, out_up = run_lane(
            step_index,
            down_total,
            from_below,
            cost_volume,
            penalty_up,
            small_pens[3],
            count_y - 1 - index_y,
            pieces,
            True,
        )
        return (down_total, send_down(out_down), send_up(out_up))

    def row_paths(step_index, carried):
        return horizontal(step_index, carried[0], carried[1], carried[2])

    def column_paths(step_index, carried):
        return vertical(step_index, carried[0], carried[1], carried[2])

    across = lax.fori_loop(0, count_x + pieces - 1, row_paths, (across, start_rows, start_rows))[0]
    down_total = lax.fori_loop(
        0, count_y + pieces - 1, column_paths, (down_total, start_cols, start_cols)
    )[0]
    return (down_total + jnp.transpose(across, (1, 0, 2))) * OUT_SCALE


def solution(mesh):
    in_specs = (P("gy", "gx", None), P("gy", "gx"), P(), P())
    out_specs = P("gy", "gx", None)
    return jax.shard_map(
        on_device, mesh=mesh, in_specs=in_specs, out_specs=out_specs, check_vma=False
    )
```

profile of v0, /device:TPU:14, one launch (start us, length us, event | category | flops | bytes accessed | tf_op | source)
XLA Modules:
  0.0 330.0 jit_solution(10913524025453232545)
XLA Ops:
  2.1 4.5 %collective-permute-start.5 = (f32[1,16]{0,1:T(8,128)S(1)}, f32[1,16]{0,1:T(8,128)S(1)}, u32[]{:S(2)}, u32[]{:S(2)}) collective-permute-start(f32[1,16]{0,1:T(8,128)S(1)} %get-tuple-element.906), channel_id=1, source_target_pairs={{8,0},{16,8},{24,16},{9,1},{17,9},{25,17},{10,2},{18,10},{26,18},{... | collective-permute-start | bytes 200 | tf_op jit(solution)/shard_map/ppermute | solution.py:27
  17.1 3.6 %collective-permute-start.7 = (f32[18,1]{0,1:T(1,128)S(1)}, f32[18,1]{0,1:T(1,128)S(1)}, u32[]{:S(2)}, u32[]{:S(2)}) collective-permute-start(f32[18,1]{0,1:T(1,128)S(1)} %get-tuple-element.903), channel_id=1, source_target_pairs={{1,0},{2,1},{3,2},{4,3},{5,4},{6,5},{7,6},{9,8},{10,9},{11,10},{12... | collective-permute-start | bytes 224 | tf_op jit(solution)/shard_map/ppermute | solution.py:27
  24.3 164.2 %while.99 = (s32[]{:T(128)}, f32[16,16,256]{2,1,0:T(8,128)S(1)}, f32[16,256]{1,0:T(8,128)S(1)}, f32[16,256]{1,0:T(8,128)S(1)}, s32[]{:T(128)}, /*index=5*/s32[]{...) while((s32[]{:T(128)}, f32[16,16,256]{2,1,0:T(8,128)S(1)}, ...), condition=%wide.region_23.24_spmd, body=%wide.region_12.23_spmd.sunk | while | flops 196625 | bytes 2264831 | solution.py:167
  29.9 4.0 %collective-permute-done = f32[16,256]{1,0:T(8,128)S(1)} collective-permute-done((f32[16,256]{1,0:T(8,128)S(1)}, f32[16,256]{1,0:T(8,128)S(1)}, u32[]{:S(2)}, u32[]{:S(2)}) %collective-permute-start) | collective-permute-done | bytes 16416 | tf_op jit(solution)/shard_map/while/body/eval_jaxpr/ppermute | solution.py:16
  34.0 6.1 %collective-permute-start.1 = (f32[16,256]{1,0:T(8,128)S(1)}, f32[16,256]{1,0:T(8,128)S(1)}, u32[]{:S(2)}, u32[]{:S(2)}) collective-permute-start(f32[16,256]{1,0:T(8,128)S(1)} %get-tuple-element.1185), channel_id=1, source_target_pairs={{1,0},{2,1},{3,2},{4,3},{5,4},{6,5},{7,6},{9,8},{10,9},{11,10},{12... | collective-permute-start | bytes 49160 | tf_op jit(solution)/shard_map/while/body/eval_jaxpr/ppermute | solution.py:16
  45.2 4.4 %conditional.10 = (f32[16,16,256]{2,1,0:T(8,128)S(1)}, f32[16,256]{1,0:T(8,128)S(1)}) conditional(s32[]{:T(128)} %convert_element_type.91, f32[16,16,256]{2,1,0:T(8,128)S(1)} %get-tuple-element.1385, (f32[4]{0:T(128)S(1)}, s32[16,16,256]{2,1,0:T(8,128)S(1)}, f32[16,16]{1,0:T(8,128)S(1)}, f32[16,256]{1,0:T(8,128)S(1)}, ...), branch_computations={%region_13.13_spmd, %region_14.17_spmd} | conditional | flops 98306 | bytes 935865 | solution.py:85
  45.2 4.3 %while.96 = (s32[]{:T(128)}, f32[16,256]{1,0:T(8,128)S(1)}, f32[16,16,256]{2,1,0:T(8,128)S(1)}, s32[16,16,256]{2,1,0:T(8,128)S(1)}, f32[]{:T(128)S(1)}, /*index=5*/f32[16,16]{1,0:T(8,128)S(1)}, s32[]{:T(128)}, f32[]{:T(128)}) while((s32[]{:T(128)}, f32[16,256]{1,0:T(8,128)S(1)}, f32[16,16,256]{2,1,0:T(8,128)S(1)}, ...), condition=%wide.region_17.16_spmd, body=%wide.region_15.15_spmd.sunk | while | flops 32770 | bytes 116577 | solution.py:43
  58.6 4.9 %collective-permute-start = (f32[16,256]{1,0:T(8,128)S(1)}, f32[16,256]{1,0:T(8,128)S(1)}, u32[]{:S(2)}, u32[]{:S(2)}) collective-permute-start(f32[16,256]{1,0:T(8,128)S(1)} %get-tuple-element.1184), channel_id=1, source_target_pairs={{0,1},{1,2},{2,3},{3,4},{4,5},{5,6},{6,7},{8,9},{9,10},{10,11},{11... | collective-permute-start | bytes 49160 | tf_op jit(solution)/shard_map/while/body/eval_jaxpr/ppermute | solution.py:16
  66.2 58.5 %collective-permute-start = (f32[16,256]{1,0:T(8,128)S(1)}, f32[16,256]{1,0:T(8,128)S(1)}, u32[]{:S(2)}, u32[]{:S(2)}) collective-permute-start(f32[16,256]{1,0:T(8,128)S(1)} %get-tuple-element.1184), channel_id=1, source_target_pairs={{0,1},{1,2},{2,3},{3,4},{4,5},{5,6},{6,7},{8,9},{9,10},{10,11},{11... | collective-permute-start | bytes 49160 | tf_op jit(solution)/shard_map/while/body/eval_jaxpr/ppermute | solution.py:16
  125.6 15.3 %conditional.11 = (f32[16,16,256]{2,1,0:T(8,128)S(1)}, f32[16,256]{1,0:T(8,128)S(1)}) conditional(s32[]{:T(128)} %convert_element_type.90, f32[16,16,256]{2,1,0:T(8,128)S(1)} %get-tuple-element.1182, (f32[4]{0:T(128)S(1)}, s32[16,16,256]{2,1,0:T(8,128)S(1)}, f32[16,16]{1,0:T(8,128)S(1)}, f32[16,256]{1,0:T(8,128)S(1)}, ...), branch_computations={%region_18.18_spmd, %region_19.22_spmd} | conditional | flops 98307 | bytes 1197541 | solution.py:85
  126.2 14.6 %while.97 = (s32[]{:T(128)}, f32[16,256]{1,0:T(8,128)S(1)}, f32[16,16,256]{2,1,0:T(8,128)S(1)}, s32[16,16,256]{2,1,0:T(8,128)S(1)}, f32[]{:T(128)}, /*index=5*/f...) while((s32[]{:T(128)}, f32[16,256]{1,0:T(8,128)S(1)}, f32[16,16,256]{2,1,0:T(8,128)S(1)}, ...), condition=%wide.region_22.21_spmd, body=%wide.region_20.20_spmd.sunk | while | flops 32771 | bytes 116089 | solution.py:43
  147.9 16.7 %collective-permute-start.1 = (f32[16,256]{1,0:T(8,128)S(1)}, f32[16,256]{1,0:T(8,128)S(1)}, u32[]{:S(2)}, u32[]{:S(2)}) collective-permute-start(f32[16,256]{1,0:T(8,128)S(1)} %get-tuple-element.1185), channel_id=1, source_target_pairs={{1,0},{2,1},{3,2},{4,3},{5,4},{6,5},{7,6},{9,8},{10,9},{11,10},{12... | collective-permute-start | bytes 49160 | tf_op jit(solution)/shard_map/while/body/eval_jaxpr/ppermute | solution.py:16
  174.1 14.4 %collective-permute-done = f32[16,256]{1,0:T(8,128)S(1)} collective-permute-done((f32[16,256]{1,0:T(8,128)S(1)}, f32[16,256]{1,0:T(8,128)S(1)}, u32[]{:S(2)}, u32[]{:S(2)}) %collective-permute-start) | collective-permute-done | bytes 16416 | tf_op jit(solution)/shard_map/while/body/eval_jaxpr/ppermute | solution.py:16
  188.6 140.6 %while.98 = (s32[]{:T(128)}, f32[16,16,256]{2,1,0:T(8,128)S(1)}, f32[16,256]{1,0:T(8,128)S(1)}, f32[16,256]{1,0:T(8,128)S(1)}, s32[]{:T(128)}, /*index=5*/s32[]{...) while((s32[]{:T(128)}, f32[16,16,256]{2,1,0:T(8,128)S(1)}, ...), condition=%wide.region_11.12_spmd, body=%wide.region_0.11_spmd.sunk | while | flops 196625 | bytes 2264331 | solution.py:168
  188.6 26.1 %conditional.9 = (f32[16,16,256]{2,1,0:T(8,128)S(1)}, f32[16,256]{1,0:T(8,128)S(1)}) conditional(s32[]{:T(128)} %convert_element_type.88, f32[16,16,256]{2,1,0:T(8,128)S(1)} %get-tuple-element.1168, (f32[4]{0:T(128)S(1)}, s32[16,16,256]{2,1,0:T(8,128)}, f32[16,16]{1,0:T(8,128)S(1)}, f32[16,256]{1,0:T(8,128)S(1)}, f32[16,16,256]{2,1,0:T(8,128)S(1)}) %tuple.210), branch_computations={%region_6.6_spmd, %region_7.10_spmd} | conditional | flops 98307 | bytes 1197541 | solution.py:85
  189.3 25.3 %while.95 = (s32[]{:T(128)}, f32[16,256]{1,0:T(8,128)S(1)}, f32[16,16,256]{2,1,0:T(8,128)S(1)}, s32[16,16,256]{2,1,0:T(8,128)}, f32[]{:T(128)}, /*index=5*/f32[16,16]{1,0:T(8,128)S(1)}, s32[]{:T(128)}, s32[]{:T(128)}, f32[]{:T(128)}) while((s32[]{:T(128)}, f32[16,256]{1,0:T(8,128)S(1)}, f32[16,16,256]{2,1,0:T(8,128)S(1)}, ...), condition=%wide.region_10.9_spmd, body=%wide.region_8.8_spmd.sunk | while | flops 32771 | bytes 116089 | solution.py:43
  217.4 4.2 %collective-permute-done.2 = f32[16,256]{1,0:T(8,128)S(1)} collective-permute-done((f32[16,256]{1,0:T(8,128)S(1)}, f32[16,256]{1,0:T(8,128)S(1)}, u32[]{:S(2)}, u32[]{:S(2)}) %collective-permute-start.2) | collective-permute-done | bytes 16416 | tf_op jit(solution)/shard_map/while/body/eval_jaxpr/ppermute | solution.py:16
  221.6 29.0 %collective-permute-start.3 = (f32[16,256]{1,0:T(8,128)S(1)}, f32[16,256]{1,0:T(8,128)S(1)}, u32[]{:S(2)}, u32[]{:S(2)}) collective-permute-start(f32[16,256]{1,0:T(8,128)S(1)} %get-tuple-element.1171), channel_id=1, source_target_pairs={{8,0},{16,8},{24,16},{9,1},{17,9},{25,17},{10,2},{18,10},{26,18},{... | collective-permute-start | bytes 49160 | tf_op jit(solution)/shard_map/while/body/eval_jaxpr/ppermute | solution.py:16
  252.1 5.3 %collective-permute-done.2 = f32[16,256]{1,0:T(8,128)S(1)} collective-permute-done((f32[16,256]{1,0:T(8,128)S(1)}, f32[16,256]{1,0:T(8,128)S(1)}, u32[]{:S(2)}, u32[]{:S(2)}) %collective-permute-start.2) | collective-permute-done | bytes 16416 | tf_op jit(solution)/shard_map/while/body/eval_jaxpr/ppermute | solution.py:16
  257.4 32.0 %collective-permute-start.3 = (f32[16,256]{1,0:T(8,128)S(1)}, f32[16,256]{1,0:T(8,128)S(1)}, u32[]{:S(2)}, u32[]{:S(2)}) collective-permute-start(f32[16,256]{1,0:T(8,128)S(1)} %get-tuple-element.1171), channel_id=1, source_target_pairs={{8,0},{16,8},{24,16},{9,1},{17,9},{25,17},{10,2},{18,10},{26,18},{... | collective-permute-start | bytes 49160 | tf_op jit(solution)/shard_map/while/body/eval_jaxpr/ppermute | solution.py:16
  290.8 4.2 %collective-permute-done.2 = f32[16,256]{1,0:T(8,128)S(1)} collective-permute-done((f32[16,256]{1,0:T(8,128)S(1)}, f32[16,256]{1,0:T(8,128)S(1)}, u32[]{:S(2)}, u32[]{:S(2)}) %collective-permute-start.2) | collective-permute-done | bytes 16416 | tf_op jit(solution)/shard_map/while/body/eval_jaxpr/ppermute | solution.py:16
  295.0 27.1 %conditional.8 = (f32[16,16,256]{2,1,0:T(8,128)S(1)}, f32[16,256]{1,0:T(8,128)S(1)}) conditional(s32[]{:T(128)} %convert_element_type.89, f32[16,16,256]{2,1,0:T(8,128)S(1)} %get-tuple-element.1349, (f32[4]{0:T(128)S(1)}, s32[16,16,256]{2,1,0:T(8,128)}, f32[16,16]{1,0:T(8,128)S(1)}, f32[16,256]{1,0:T(8,128)S(1)}, f32[16,16,256]{2,1,0:T(8,128)S(1)}) %tuple.209), branch_computations={%region_1.0_spmd, %region_2.5_spmd} | conditional | flops 98306 | bytes 935365 | solution.py:85
  295.7 26.4 %while.94 = (s32[]{:T(128)}, f32[16,256]{1,0:T(8,128)S(1)}, f32[16,16,256]{2,1,0:T(8,128)S(1)}, s32[16,16,256]{2,1,0:T(8,128)}, f32[]{:T(128)}, /*index=5*/f32[16,16]{1,0:T(8,128)S(1)}, s32[]{:T(128)}, f32[]{:T(128)}) while((s32[]{:T(128)}, f32[16,256]{1,0:T(8,128)S(1)}, f32[16,16,256]{2,1,0:T(8,128)S(1)}, s32[16,16,256]{2,1,0:T(8,128)}, ...), condition=%wide.region_5.4_spmd, body=%wide.region_3.3_spmd.sunk | while | flops 32770 | bytes 116069 | solution.py:43
  324.9 4.2 %collective-permute-done.2 = f32[16,256]{1,0:T(8,128)S(1)} collective-permute-done((f32[16,256]{1,0:T(8,128)S(1)}, f32[16,256]{1,0:T(8,128)S(1)}, u32[]{:S(2)}, u32[]{:S(2)}) %collective-permute-start.2) | collective-permute-done | bytes 16416 | tf_op jit(solution)/shard_map/while/body/eval_jaxpr/ppermute | solution.py:16
  (376 shorter events, 130.2 us)
Async XLA Ops:
  0.8 14.2 %collective-permute-start.4 = (f32[1,16]{0,1:T(8,128)S(1)}, f32[1,16]{0,1:T(8,128)S(1)}, u32[]{:S(2)}, u32[]{:S(2)}) collective-permute-start(f32[1,16]{0,1:T(8,128)S(1)} %get-tuple-element.907), channel_id=1, source_target_pairs={{0,8},{8,16},{16,24},{1,9},{9,17},{17,25},{2,10},{10,18},{18,26},{... | collective-permute-start | bytes 200 | tf_op jit(solution)/shard_map/ppermute | solution.py:24
  2.1 12.9 %collective-permute-start.5 = (f32[1,16]{0,1:T(8,128)S(1)}, f32[1,16]{0,1:T(8,128)S(1)}, u32[]{:S(2)}, u32[]{:S(2)}) collective-permute-start(f32[1,16]{0,1:T(8,128)S(1)} %get-tuple-element.906), channel_id=1, source_target_pairs={{8,0},{16,8},{24,16},{9,1},{17,9},{25,17},{10,2},{18,10},{26,18},{... | collective-permute-start | bytes 200 | tf_op jit(solution)/shard_map/ppermute | solution.py:27
  15.2 6.4 %collective-permute-start.6 = (f32[18,1]{0,1:T(1,128)S(1)}, f32[18,1]{0,1:T(1,128)S(1)}, u32[]{:S(2)}, u32[]{:S(2)}) collective-permute-start(f32[18,1]{0,1:T(1,128)S(1)} %get-tuple-element.904), channel_id=1, source_target_pairs={{0,1},{1,2},{2,3},{3,4},{4,5},{5,6},{6,7},{8,9},{9,10},{10,11},{11... | collective-permute-start | bytes 224 | tf_op jit(solution)/shard_map/ppermute | solution.py:24
  17.1 4.9 %collective-permute-start.7 = (f32[18,1]{0,1:T(1,128)S(1)}, f32[18,1]{0,1:T(1,128)S(1)}, u32[]{:S(2)}, u32[]{:S(2)}) collective-permute-start(f32[18,1]{0,1:T(1,128)S(1)} %get-tuple-element.903), channel_id=1, source_target_pairs={{1,0},{2,1},{3,2},{4,3},{5,4},{6,5},{7,6},{9,8},{10,9},{11,10},{12... | collective-permute-start | bytes 224 | tf_op jit(solution)/shard_map/ppermute | solution.py:27
  24.4 5.5 %collective-permute-start.1 = (f32[16,256]{1,0:T(8,128)S(1)}, f32[16,256]{1,0:T(8,128)S(1)}, u32[]{:S(2)}, u32[]{:S(2)}) collective-permute-start(f32[16,256]{1,0:T(8,128)S(1)} %get-tuple-element.1185), channel_id=1, source_target_pairs={{1,0},{2,1},{3,2},{4,3},{5,4},{6,5},{7,6},{9,8},{10,9},{11,10},{12... | collective-permute-start | bytes 49160 | tf_op jit(solution)/shard_map/while/body/eval_jaxpr/ppermute | solution.py:16
  28.0 6.0 %collective-permute-start = (f32[16,256]{1,0:T(8,128)S(1)}, f32[16,256]{1,0:T(8,128)S(1)}, u32[]{:S(2)}, u32[]{:S(2)}) collective-permute-start(f32[16,256]{1,0:T(8,128)S(1)} %get-tuple-element.1184), channel_id=1, source_target_pairs={{0,1},{1,2},{2,3},{3,4},{4,5},{5,6},{6,7},{8,9},{9,10},{10,11},{11... | collective-permute-start | bytes 49160 | tf_op jit(solution)/shard_map/while/body/eval_jaxpr/ppermute | solution.py:16
  34.0 8.1 %collective-permute-start.1 = (f32[16,256]{1,0:T(8,128)S(1)}, f32[16,256]{1,0:T(8,128)S(1)}, u32[]{:S(2)}, u32[]{:S(2)}) collective-permute-start(f32[16,256]{1,0:T(8,128)S(1)} %get-tuple-element.1185), channel_id=1, source_target_pairs={{1,0},{2,1},{3,2},{4,3},{5,4},{6,5},{7,6},{9,8},{10,9},{11,10},{12... | collective-permute-start | bytes 49160 | tf_op jit(solution)/shard_map/while/body/eval_jaxpr/ppermute | solution.py:16
  40.1 5.1 %collective-permute-start = (f32[16,256]{1,0:T(8,128)S(1)}, f32[16,256]{1,0:T(8,128)S(1)}, u32[]{:S(2)}, u32[]{:S(2)}) collective-permute-start(f32[16,256]{1,0:T(8,128)S(1)} %get-tuple-element.1184), channel_id=1, source_target_pairs={{0,1},{1,2},{2,3},{3,4},{4,5},{5,6},{6,7},{8,9},{9,10},{10,11},{11... | collective-permute-start | bytes 49160 | tf_op jit(solution)/shard_map/while/body/eval_jaxpr/ppermute | solution.py:16
  49.7 4.3 %collective-permute-start.1 = (f32[16,256]{1,0:T(8,128)S(1)}, f32[16,256]{1,0:T(8,128)S(1)}, u32[]{:S(2)}, u32[]{:S(2)}) collective-permute-start(f32[16,256]{1,0:T(8,128)S(1)} %get-tuple-element.1185), channel_id=1, source_target_pairs={{1,0},{2,1},{3,2},{4,3},{5,4},{6,5},{7,6},{9,8},{10,9},{11,10},{12... | collective-permute-start | bytes 49160 | tf_op jit(solution)/shard_map/while/body/eval_jaxpr/ppermute | solution.py:16
  51.6 5.1 %collective-permute-start = (f32[16,256]{1,0:T(8,128)S(1)}, f32[16,256]{1,0:T(8,128)S(1)}, u32[]{:S(2)}, u32[]{:S(2)}) collective-permute-start(f32[16,256]{1,0:T(8,128)S(1)} %get-tuple-element.1184), channel_id=1, source_target_pairs={{0,1},{1,2},{2,3},{3,4},{4,5},{5,6},{6,7},{8,9},{9,10},{10,11},{11... | collective-permute-start | bytes 49160 | tf_op jit(solution)/shard_map/while/body/eval_jaxpr/ppermute | solution.py:16
  56.6 6.9 %collective-permute-start.1 = (f32[16,256]{1,0:T(8,128)S(1)}, f32[16,256]{1,0:T(8,128)S(1)}, u32[]{:S(2)}, u32[]{:S(2)}) collective-permute-start(f32[16,256]{1,0:T(8,128)S(1)} %get-tuple-element.1185), channel_id=1, source_target_pairs={{1,0},{2,1},{3,2},{4,3},{5,4},{6,5},{7,6},{9,8},{10,9},{11,10},{12... | collective-permute-start | bytes 49160 | tf_op jit(solution)/shard_map/while/body/eval_jaxpr/ppermute | solution.py:16
  58.6 5.7 %collective-permute-start = (f32[16,256]{1,0:T(8,128)S(1)}, f32[16,256]{1,0:T(8,128)S(1)}, u32[]{:S(2)}, u32[]{:S(2)}) collective-permute-start(f32[16,256]{1,0:T(8,128)S(1)} %get-tuple-element.1184), channel_id=1, source_target_pairs={{0,1},{1,2},{2,3},{3,4},{4,5},{5,6},{6,7},{8,9},{9,10},{10,11},{11... | collective-permute-start | bytes 49160 | tf_op jit(solution)/shard_map/while/body/eval_jaxpr/ppermute | solution.py:16
  64.3 60.4 %collective-permute-start.1 = (f32[16,256]{1,0:T(8,128)S(1)}, f32[16,256]{1,0:T(8,128)S(1)}, u32[]{:S(2)}, u32[]{:S(2)}) collective-permute-start(f32[16,256]{1,0:T(8,128)S(1)} %get-tuple-element.1185), channel_id=1, source_target_pairs={{1,0},{2,1},{3,2},{4,3},{5,4},{6,5},{7,6},{9,8},{10,9},{11,10},{12... | collective-permute-start | bytes 49160 | tf_op jit(solution)/shard_map/while/body/eval_jaxpr/ppermute | solution.py:16
  66.2 59.3 %collective-permute-start = (f32[16,256]{1,0:T(8,128)S(1)}, f32[16,256]{1,0:T(8,128)S(1)}, u32[]{:S(2)}, u32[]{:S(2)}) collective-permute-start(f32[16,256]{1,0:T(8,128)S(1)} %get-tuple-element.1184), channel_id=1, source_target_pairs={{0,1},{1,2},{2,3},{3,4},{4,5},{5,6},{6,7},{8,9},{9,10},{10,11},{11... | collective-permute-start | bytes 49160 | tf_op jit(solution)/shard_map/while/body/eval_jaxpr/ppermute | solution.py:16
  142.9 5.1 %collective-permute-start = (f32[16,256]{1,0:T(8,128)S(1)}, f32[16,256]{1,0:T(8,128)S(1)}, u32[]{:S(2)}, u32[]{:S(2)}) collective-permute-start(f32[16,256]{1,0:T(8,128)S(1)} %get-tuple-element.1184), channel_id=1, source_target_pairs={{0,1},{1,2},{2,3},{3,4},{4,5},{5,6},{6,7},{8,9},{9,10},{10,11},{11... | collective-permute-start | bytes 49160 | tf_op jit(solution)/shard_map/while/body/eval_jaxpr/ppermute | solution.py:16
  147.9 18.7 %collective-permute-start.1 = (f32[16,256]{1,0:T(8,128)S(1)}, f32[16,256]{1,0:T(8,128)S(1)}, u32[]{:S(2)}, u32[]{:S(2)}) collective-permute-start(f32[16,256]{1,0:T(8,128)S(1)} %get-tuple-element.1185), channel_id=1, source_target_pairs={{1,0},{2,1},{3,2},{4,3},{5,4},{6,5},{7,6},{9,8},{10,9},{11,10},{12... | collective-permute-start | bytes 49160 | tf_op jit(solution)/shard_map/while/body/eval_jaxpr/ppermute | solution.py:16
  164.6 5.1 %collective-permute-start = (f32[16,256]{1,0:T(8,128)S(1)}, f32[16,256]{1,0:T(8,128)S(1)}, u32[]{:S(2)}, u32[]{:S(2)}) collective-permute-start(f32[16,256]{1,0:T(8,128)S(1)} %get-tuple-element.1184), channel_id=1, source_target_pairs={{0,1},{1,2},{2,3},{3,4},{4,5},{5,6},{6,7},{8,9},{9,10},{10,11},{11... | collective-permute-start | bytes 49160 | tf_op jit(solution)/shard_map/while/body/eval_jaxpr/ppermute | solution.py:16
  171.6 16.9 %collective-permute-start = (f32[16,256]{1,0:T(8,128)S(1)}, f32[16,256]{1,0:T(8,128)S(1)}, u32[]{:S(2)}, u32[]{:S(2)}) collective-permute-start(f32[16,256]{1,0:T(8,128)S(1)} %get-tuple-element.1184), channel_id=1, source_target_pairs={{0,1},{1,2},{2,3},{3,4},{4,5},{5,6},{6,7},{8,9},{9,10},{10,11},{11... | collective-permute-start | bytes 49160 | tf_op jit(solution)/shard_map/while/body/eval_jaxpr/ppermute | solution.py:16
  216.0 5.6 %collective-permute-start.2 = (f32[16,256]{1,0:T(8,128)S(1)}, f32[16,256]{1,0:T(8,128)S(1)}, u32[]{:S(2)}, u32[]{:S(2)}) collective-permute-start(f32[16,256]{1,0:T(8,128)S(1)} %get-tuple-element.1170), channel_id=1, source_target_pairs={{0,8},{8,16},{16,24},{1,9},{9,17},{17,25},{2,10},{10,18},{18,26},{... | collective-permute-start | bytes 49160 | tf_op jit(solution)/shard_map/while/body/eval_jaxpr/ppermute | solution.py:16
  221.6 30.4 %collective-permute-start.3 = (f32[16,256]{1,0:T(8,128)S(1)}, f32[16,256]{1,0:T(8,128)S(1)}, u32[]{:S(2)}, u32[]{:S(2)}) collective-permute-start(f32[16,256]{1,0:T(8,128)S(1)} %get-tuple-element.1171), channel_id=1, source_target_pairs={{8,0},{16,8},{24,16},{9,1},{17,9},{25,17},{10,2},{18,10},{26,18},{... | collective-permute-start | bytes 49160 | tf_op jit(solution)/shard_map/while/body/eval_jaxpr/ppermute | solution.py:16
  250.6 6.7 %collective-permute-start.2 = (f32[16,256]{1,0:T(8,128)S(1)}, f32[16,256]{1,0:T(8,128)S(1)}, u32[]{:S(2)}, u32[]{:S(2)}) collective-permute-start(f32[16,256]{1,0:T(8,128)S(1)} %get-tuple-element.1170), channel_id=1, source_target_pairs={{0,8},{8,16},{16,24},{1,9},{9,17},{17,25},{2,10},{10,18},{18,26},{... | collective-permute-start | bytes 49160 | tf_op jit(solution)/shard_map/while/body/eval_jaxpr/ppermute | solution.py:16
  257.4 33.4 %collective-permute-start.3 = (f32[16,256]{1,0:T(8,128)S(1)}, f32[16,256]{1,0:T(8,128)S(1)}, u32[]{:S(2)}, u32[]{:S(2)}) collective-permute-start(f32[16,256]{1,0:T(8,128)S(1)} %get-tuple-element.1171), channel_id=1, source_target_pairs={{8,0},{16,8},{24,16},{9,1},{17,9},{25,17},{10,2},{18,10},{26,18},{... | collective-permute-start | bytes 49160 | tf_op jit(solution)/shard_map/while/body/eval_jaxpr/ppermute | solution.py:16
  289.4 5.6 %collective-permute-start.2 = (f32[16,256]{1,0:T(8,128)S(1)}, f32[16,256]{1,0:T(8,128)S(1)}, u32[]{:S(2)}, u32[]{:S(2)}) collective-permute-start(f32[16,256]{1,0:T(8,128)S(1)} %get-tuple-element.1170), channel_id=1, source_target_pairs={{0,8},{8,16},{16,24},{1,9},{9,17},{17,25},{2,10},{10,18},{18,26},{... | collective-permute-start | bytes 49160 | tf_op jit(solution)/shard_map/while/body/eval_jaxpr/ppermute | solution.py:16
  323.5 5.6 %collective-permute-start.2 = (f32[16,256]{1,0:T(8,128)S(1)}, f32[16,256]{1,0:T(8,128)S(1)}, u32[]{:S(2)}, u32[]{:S(2)}) collective-permute-start(f32[16,256]{1,0:T(8,128)S(1)} %get-tuple-element.1170), channel_id=1, source_target_pairs={{0,8},{8,16},{16,24},{1,9},{9,17},{17,25},{2,10},{10,18},{18,26},{... | collective-permute-start | bytes 49160 | tf_op jit(solution)/shard_map/while/body/eval_jaxpr/ppermute | solution.py:16
  (6 other events, 15.5 us)
where the time goes:
time: 334 us; the launch traced here: 330 us
  starting transfers between devices  193 us (58%)
  other arithmetic  72.4 us (22%)
  waiting for transfers between devices  50.5 us (15%)
  local copies, waits for them, and re-layouts  6.34 us (2%)
  between operations  5.36 us (2%)
    ppermute x24, starting transfers between devices, shifted(): return lax.ppermute(shard, axis, pairs)  181 us
    dynamic_update_slice x64, other arithmetic, sweep(): lax.scan(partial(advance, penalty_one=penalty_one), start, (cost_lines, l...  60.3 us
    ppermute x24, waiting for transfers between devices, shifted(): return lax.ppermute(shard, axis, pairs)  50 us
    ppermute x2, starting transfers between devices, padded_2(): lax.ppermute(lax.slice_in_dim(block, 0, width, axis=dim), axis, backward)  8.19 us
    reduce_min x64, other arithmetic, advance(): lowest = jnp.min(previous, axis=-1, keepdims=True)  7.41 us
  transfers between devices with their start and end apart: 28, of which 17 were waited for; matrix products, arithmetic and copies ran while one was open for 1% of the time, Pallas kernels for 0%

commit v1 on v0

v1 whole, which is shorter than its diff:
```python
import functools

import jax
import jax.numpy as jnp
from jax import lax
from jax.experimental import pallas as pl
from jax.experimental.pallas import tpu as pltpu
from jax.sharding import PartitionSpec as P

FAR = 1e30
GRADIENT_GAIN = 4.0
OUT_SCALE = 1.0 / 256.0
LANES = 128
SUBLANES = 8
MESH = pl.DeviceIdType.MESH


def tree_min(parts):
    parts = list(parts)
    while len(parts) > 1:
        pairs = [jnp.minimum(a, b) for a, b in zip(parts[::2], parts[1::2])]
        parts = pairs + ([parts[-1]] if len(parts) % 2 else [])
    return parts[0]


def all_sublanes_min(x):
    for by in (4, 2, 1):
        x = jnp.minimum(x, pltpu.roll(x, by, 0))
    return x


def kernel(
    rows,
    cols,
    cost_ref,
    image_ref,
    small_ref,
    large_ref,
    out_ref,
    staged,
    totals,
    costs,
    paths,
    turned,
    large_lines,
    image_lines,
    outbox,
    inbox,
    edge_out,
    edge_in,
    send_sems,
    recv_sems,
    edge_send_sems,
    edge_recv_sems,
    local_sems,
):
    disparities = cost_ref.shape[1]
    nv = disparities // SUBLANES
    nx, ny = lax.axis_size("gx"), lax.axis_size("gy")
    ix, iy = lax.axis_index("gx"), lax.axis_index("gy")
    lines = (rows, rows, cols, cols)
    lengths = (cols, cols, rows, rows)
    backward = (False, True, False, True)
    targets = (
        {"gx": ix + 1},
        {"gx": ix - 1},
        {"gy": iy + 1},
        {"gy": iy - 1},
    )
    has_next = (ix < nx - 1, ix > 0, iy < ny - 1, iy > 0)
    has_prev = (ix > 0, ix < nx - 1, iy > 0, iy < ny - 1)

    halves = disparities // LANES

    def cost_copy(h):
        return pltpu.make_async_copy(
            cost_ref.at[:, pl.ds(h * LANES, LANES)], staged.at[h], local_sems.at[h]
        )

    def total_copy(h):
        return pltpu.make_async_copy(
            totals.at[h], out_ref.at[:, pl.ds(h * LANES, LANES)], local_sems.at[h]
        )

    for h in range(halves):
        cost_copy(h).start()

    barrier = pltpu.get_barrier_semaphore()
    for k in range(4):

        @pl.when(has_next[k])
        def _(k=k):
            pl.semaphore_signal(barrier, inc=1, device_id=targets[k], device_id_type=MESH)

    neighbours = sum(jnp.where(flag, 1, 0) for flag in has_next)

    image = image_ref[...]
    image_lines[...] = jnp.zeros_like(image_lines)
    image_lines[0, :cols, :rows] = image.T
    image_lines[1, :rows, :cols] = image
    edge_out[...] = jnp.zeros_like(edge_out)
    for k in range(4):
        last = 0 if backward[k] else lengths[k] - 1
        edge_out[k, 0:1, :] = image_lines[k // 2, last : last + 1, :]
    pl.semaphore_wait(barrier, neighbours)

    def edge_copy(k):
        return pltpu.make_async_remote_copy(
            src_ref=edge_out.at[k],
            dst_ref=edge_in.at[k],
            send_sem=edge_send_sems.at[k],
            recv_sem=edge_recv_sems.at[k],
            device_id=targets[k],
            device_id_type=MESH,
        )

    def path_copy(k):
        return pltpu.make_async_remote_copy(
            src_ref=outbox.at[k],
            dst_ref=inbox.at[k],
            send_sem=send_sems.at[k],
            recv_sem=recv_sems.at[k],
            device_id=targets[k],
            device_id_type=MESH,
        )

    for k in range(4):

        @pl.when(has_next[k])
        def _(k=k):
            edge_copy(k).start()

    for h in range(halves):
        cost_copy(h).wait()

    def turn_in(axis, line, at, count):
        for h in range(halves):
            block = staged[h, at, :].astype(jnp.float32)
            turned[h * LANES : (h + 1) * LANES, :count] = block.T
        for v in range(nv):
            costs[axis, line, v] = turned[pl.ds(v, SUBLANES, stride=nv), :]

    def turn_across(line, carry):
        turn_in(0, line, pl.ds(line, rows, stride=cols), rows)
        return carry

    def turn_down(line, carry):
        turn_in(1, line, pl.ds(pl.multiple_of(line * cols, cols), cols), cols)
        return carry

    lax.fori_loop(0, cols, turn_across, 0)
    lax.fori_loop(0, rows, turn_down, 0)

    sub = lax.broadcasted_iota(jnp.int32, (SUBLANES, LANES), 0)
    lane = lax.broadcasted_iota(jnp.int32, (SUBLANES, LANES), 1)

    def task(k):
        axis = k // 2
        length, width = lengths[k], lines[k]
        group = LANES // width
        small = small_ref[k].astype(jnp.float32)
        large = large_ref[k].astype(jnp.float32)
        own = image_lines[axis, :length, :]

        @pl.when(has_prev[k])
        def _():
            edge_copy(k).wait_recv()

        @pl.when(jnp.logical_not(has_prev[k]))
        def _():
            edge_in[k] = jnp.zeros((SUBLANES, LANES), jnp.float32)
            inbox[k] = jnp.zeros(inbox.shape[1:], jnp.float32)

        edge = edge_in[k, 0:1, :]
        if backward[k]:
            before = jnp.concatenate([own[1:], edge], axis=0)
        else:
            before = jnp.concatenate([edge, own[:-1]], axis=0)
        large_lines[k] = small + (large - small) / (1.0 + GRADIENT_GAIN * jnp.abs(own - before))

        @pl.when(has_prev[k])
        def _():
            path_copy(k).wait_recv()

        state = []
        for v in range(nv):
            packed = inbox[k, v // group]
            shift = (v % group) * width
            state.append(pltpu.roll(packed, LANES - shift, 1) if shift else packed)

        def step(index, state):
            line = length - 1 - index if backward[k] else index
            capped = large_lines[k, pl.ds(line, SUBLANES, stride=0), :]
            lowest = all_sublanes_min(tree_min(state))
            under = jnp.where(sub == 0, FAR, pltpu.roll(state[-1], 1, 0))
            over = jnp.where(sub == SUBLANES - 1, FAR, pltpu.roll(state[0], SUBLANES - 1, 0))
            fresh = []
            for v in range(nv):
                low = state[v - 1] if v else under
                high = state[v + 1] if v < nv - 1 else over
                near = jnp.minimum(state[v], jnp.minimum(low, high) + small)
                value = costs[axis, line, v] + jnp.minimum(near - lowest, capped)
                paths[k, line, v] = value
                fresh.append(value)
            return tuple(fresh)

        state = lax.fori_loop(0, length, step, tuple(state))

        @pl.when(has_next[k])
        def _():
            for slot in range(nv // group):
                packed = state[slot * group]
                for g in range(1, group):
                    moved = pltpu.roll(state[slot * group + g], g * width, 1)
                    packed = jnp.where(lane >= g * width, moved, packed)
                outbox[k, slot] = packed
            path_copy(k).start()

    def turn_out(k, line, count):
        for v in range(nv):
            total = paths[k, line, v] + paths[k + 1, line, v]
            turned[pl.ds(v, SUBLANES, stride=nv), :] = total
        return [
            turned[h * LANES : (h + 1) * LANES, :count].T * OUT_SCALE for h in range(halves)
        ]

    def down_total(line, carry):
        at = pl.ds(pl.multiple_of(line * cols, cols), cols)
        for h, part in enumerate(turn_out(2, line, cols)):
            totals[h, at, :] = part
        return carry

    def across_total(line, carry):
        at = pl.ds(line, rows, stride=cols)
        for h, part in enumerate(turn_out(0, line, rows)):
            totals[h, at, :] = totals[h, at, :] + part
        return carry

    low_turn = jnp.minimum(ix, nx - 1 - ix)
    high_turn = jnp.maximum(ix, nx - 1 - ix)

    def one_turn(turn, carry):
        pl.when(turn == ix)(lambda: task(0))
        pl.when(turn == nx - 1 - ix)(lambda: task(1))
        taken = jnp.logical_or(turn == low_turn, turn == high_turn)
        used = jnp.where(low_turn < turn, 1, 0) + jnp.where(high_turn < turn, 1, 0)
        free = jnp.where(taken, -1, turn - used)
        pl.when(free == iy)(lambda: task(2))
        pl.when(free == ny - 1 - iy)(lambda: task(3))

        @pl.when(free == ny)
        def _():
            lax.fori_loop(0, rows, down_total, 0)

        return carry

    lax.fori_loop(0, max(nx, ny + 3), one_turn, 0)
    lax.fori_loop(0, cols, across_total, 0)
    for h in range(halves):
        total_copy(h).start()
    for h in range(halves):
        total_copy(h).wait()

    for k in range(4):

        @pl.when(has_next[k])
        def _(k=k):
            edge_copy(k).wait_send()
            path_copy(k).wait_send()


def on_device(cost_volume, left_image, p_small, p_large):
    rows, cols, disparities = cost_volume.shape
    nv = disparities // SUBLANES
    longest = max(rows, cols)
    packed = nv * longest // LANES
    halves = disparities // LANES
    hbm = pl.BlockSpec(memory_space=pl.ANY)
    vmem = pl.BlockSpec(memory_space=pltpu.VMEM)
    smem = pl.BlockSpec(memory_space=pltpu.SMEM)
    total = pl.pallas_call(
        functools.partial(kernel, rows, cols),
        out_shape=jax.ShapeDtypeStruct((rows * cols, disparities), jnp.float32),
        in_specs=[hbm, vmem, smem, smem],
        out_specs=hbm,
        scratch_shapes=[
            pltpu.VMEM((halves, rows * cols, LANES), jnp.int32),
            pltpu.VMEM((halves, rows * cols, LANES), jnp.float32),
            pltpu.VMEM((2, longest, nv, SUBLANES, LANES), jnp.float32),
            pltpu.VMEM((4, longest, nv, SUBLANES, LANES), jnp.float32),
            pltpu.VMEM((disparities, LANES), jnp.float32),
            pltpu.VMEM((4, longest, LANES), jnp.float32),
            pltpu.VMEM((2, longest, LANES), jnp.float32),
            pltpu.VMEM((4, packed, SUBLANES, LANES), jnp.float32),
            pltpu.VMEM((4, packed, SUBLANES, LANES), jnp.float32),
            pltpu.VMEM((4, SUBLANES, LANES), jnp.float32),
            pltpu.VMEM((4, SUBLANES, LANES), jnp.float32),
            pltpu.SemaphoreType.DMA((4,)),
            pltpu.SemaphoreType.DMA((4,)),
            pltpu.SemaphoreType.DMA((4,)),
            pltpu.SemaphoreType.DMA((4,)),
            pltpu.SemaphoreType.DMA((halves,)),
        ],
        compiler_params=pltpu.CompilerParams(collective_id=0, has_side_effects=True),
    )(cost_volume.reshape(rows * cols, disparities), left_image, p_small, p_large)
    return total.reshape(rows, cols, disparities)


def solution(mesh):
    in_specs = (P("gy", "gx", None), P("gy", "gx"), P(), P())
    out_specs = P("gy", "gx", None)
    return jax.shard_map(
        on_device, mesh=mesh, in_specs=in_specs, out_specs=out_specs, check_vma=False
    )
```

time: 334 us -> 33.2 us (0.10)
  the two profiles are of different devices: /device:TPU:14 before, /device:TPU:0 now
where the time goes in v1:
time: 33.2 us; the launch traced here: 32.9 us
  Pallas kernels  31.2 us (94%)
  local copies, waits for them, and re-layouts  1.67 us (5%)
    pallas_call x1, Pallas kernels, on_device(): pl.pallas_call(functools.partial(kernel, rows, cols), out_shape=jax.Shape...  31.2 us
    unnamed x1, local copies, waits for them, and re-layouts  1.67 us

profile of v1, /device:TPU:0, one launch (start us, length us, event | category | flops | bytes accessed | tf_op | source)
XLA Modules:
  0.0 32.9 jit_solution(2657062350400455042)
XLA Ops:
  0.0 31.2 %shard_map.46 = f32[256,256]{1,0:T(8,128)} custom-call(s32[256,256]{1,0:T(8,128)} %bitcast.3, f32[16,16]{1,0:T(8,128)} %image_ref.1, s32[4]{0:T(128)} %small_ref.1, s32[4]{0:T(128)} %large_ref.1), custom_call_target="tpu_custom_call" | custom-call | tf_op jit(solution)/shard_map/pallas_call | solution.py:281
  31.2 1.7 %copy.6 = f32[16,16,256]{2,1,0:T(8,128)} copy(f32[16,16,256]{2,1,0:T(8,128)} %bitcast.2) | data formatting | bytes 524288

commit v2 on v1

--- a/solution.py
+++ b/solution.py
@@ -12,6 +12,9 @@
 OUT_SCALE = 1.0 / 256.0
 LANES = 128
 SUBLANES = 8
+BATCH = 4
+UNROLL = 2
+VMEM_BYTES = 20 << 20
 MESH = pl.DeviceIdType.MESH
 
 
@@ -77,11 +80,6 @@
             cost_ref.at[:, pl.ds(h * LANES, LANES)], staged.at[h], local_sems.at[h]
         )
 
-    def total_copy(h):
-        return pltpu.make_async_copy(
-            totals.at[h], out_ref.at[:, pl.ds(h * LANES, LANES)], local_sems.at[h]
-        )
-
     for h in range(halves):
         cost_copy(h).start()
 
@@ -133,23 +131,26 @@
     for h in range(halves):
         cost_copy(h).wait()
 
-    def turn_in(axis, line, at, count):
+    def turn_in(slot, axis, line, at, count):
         for h in range(halves):
             block = staged[h, at, :].astype(jnp.float32)
-            turned[h * LANES : (h + 1) * LANES, :count] = block.T
+            turned[slot, h * LANES : (h + 1) * LANES, :count] = block.T
         for v in range(nv):
-            costs[axis, line, v] = turned[pl.ds(v, SUBLANES, stride=nv), :]
-
-    def turn_across(line, carry):
-        turn_in(0, line, pl.ds(line, rows, stride=cols), rows)
-        return carry
-
-    def turn_down(line, carry):
-        turn_in(1, line, pl.ds(pl.multiple_of(line * cols, cols), cols), cols)
-        return carry
-
-    lax.fori_loop(0, cols, turn_across, 0)
-    lax.fori_loop(0, rows, turn_down, 0)
+            costs[axis, line, v] = turned[slot, pl.ds(v, SUBLANES, stride=nv), :]
+
+    def turn_across(index, carry):
+        for slot in range(BATCH):
+            line = index * BATCH + slot
+            turn_in(slot, 0, line, pl.ds(line, rows, stride=cols), rows)
+        return carry
+
+    def turn_down(index, carry):
+        for slot in range(BATCH):
+            line = index * BATCH + slot
+            turn_in(slot, 1, line, pl.ds(pl.multiple_of(line * cols, cols), cols), cols)
+        return carry
+
+    lax.fori_loop(0, cols // BATCH, turn_across, 0)
 
     sub = lax.broadcasted_iota(jnp.int32, (SUBLANES, LANES), 0)
     lane = lax.broadcasted_iota(jnp.int32, (SUBLANES, LANES), 1)
@@ -204,7 +205,12 @@
                 fresh.append(value)
             return tuple(fresh)
 
-        state = lax.fori_loop(0, length, step, tuple(state))
+        def steps(index, state):
+            for part in range(UNROLL):
+                state = step(index * UNROLL + part, state)
+            return state
+
+        state = lax.fori_loop(0, length // UNROLL, steps, tuple(state))
 
         @pl.when(has_next[k])
         def _():
@@ -216,50 +222,49 @@
                 outbox[k, slot] = packed
             path_copy(k).start()
 
-    def turn_out(k, line, count):
+    def turn_out(slot, k, line, count):
         for v in range(nv):
             total = paths[k, line, v] + paths[k + 1, line, v]
-            turned[pl.ds(v, SUBLANES, stride=nv), :] = total
-        return [
-            turned[h * LANES : (h + 1) * LANES, :count].T * OUT_SCALE for h in range(halves)
-        ]
-
-    def down_total(line, carry):
-        at = pl.ds(pl.multiple_of(line * cols, cols), cols)
-        for h, part in enumerate(turn_out(2, line, cols)):
-            totals[h, at, :] = part
-        return carry
-
-    def across_total(line, carry):
-        at = pl.ds(line, rows, stride=cols)
-        for h, part in enumerate(turn_out(0, line, rows)):
-            totals[h, at, :] = totals[h, at, :] + part
+            turned[slot, pl.ds(v, SUBLANES, stride=nv), :] = total
+        return [turned[slot, h * LANES : (h + 1) * LANES, :count].T for h in range(halves)]
+
+    def down_total(index, carry):
+        for slot in range(BATCH):
+            line = index * BATCH + slot
+            at = pl.ds(pl.multiple_of(line * cols, cols), cols)
+            for h, part in enumerate(turn_out(slot, 2, line, cols)):
+                totals[h, at, :] = part
+        return carry
+
+    def across_total(index, carry):
+        for slot in range(BATCH):
+            line = index * BATCH + slot
+            at = pl.ds(line, rows, stride=cols)
+            for h, part in enumerate(turn_out(slot, 0, line, rows)):
+                totals[h, at, :] = totals[h, at, :] + part
         return carry
 
     low_turn = jnp.minimum(ix, nx - 1 - ix)
     high_turn = jnp.maximum(ix, nx - 1 - ix)
+    spare = jnp.where(low_turn >= 3, low_turn - 1, 2 * nx + 2 * ny)
 
     def one_turn(turn, carry):
         pl.when(turn == ix)(lambda: task(0))
         pl.when(turn == nx - 1 - ix)(lambda: task(1))
         taken = jnp.logical_or(turn == low_turn, turn == high_turn)
-        used = jnp.where(low_turn < turn, 1, 0) + jnp.where(high_turn < turn, 1, 0)
+        taken = jnp.logical_or(taken, turn == spare)
+        used = sum(jnp.where(at < turn, 1, 0) for at in (low_turn, high_turn, spare))
         free = jnp.where(taken, -1, turn - used)
+        pl.when(free == 0)(lambda: lax.fori_loop(0, rows // BATCH, turn_down, None))
         pl.when(free == iy)(lambda: task(2))
         pl.when(free == ny - 1 - iy)(lambda: task(3))
-
-        @pl.when(free == ny)
-        def _():
-            lax.fori_loop(0, rows, down_total, 0)
-
-        return carry
-
-    lax.fori_loop(0, max(nx, ny + 3), one_turn, 0)
-    lax.fori_loop(0, cols, across_total, 0)
+        pl.when(free == ny)(lambda: lax.fori_loop(0, rows // BATCH, down_total, None))
+        return carry
+
+    lax.fori_loop(0, max(nx, ny + 4), one_turn, 0)
+    lax.fori_loop(0, cols // BATCH, across_total, 0)
     for h in range(halves):
-        total_copy(h).start()
-    for h in range(halves):
-        total_copy(h).wait()
+        out_ref[:, h * LANES : (h + 1) * LANES] = totals[h] * OUT_SCALE
 
     for k in range(4):
 
@@ -282,13 +287,13 @@
         functools.partial(kernel, rows, cols),
         out_shape=jax.ShapeDtypeStruct((rows * cols, disparities), jnp.float32),
         in_specs=[hbm, vmem, smem, smem],
-        out_specs=hbm,
+        out_specs=vmem,
         scratch_shapes=[
             pltpu.VMEM((halves, rows * cols, LANES), jnp.int32),
             pltpu.VMEM((halves, rows * cols, LANES), jnp.float32),
             pltpu.VMEM((2, longest, nv, SUBLANES, LANES), jnp.float32),
             pltpu.VMEM((4, longest, nv, SUBLANES, LANES), jnp.float32),
-            pltpu.VMEM((disparities, LANES), jnp.float32),
+            pltpu.VMEM((BATCH, disparities, LANES), jnp.float32),
             pltpu.VMEM((4, longest, LANES), jnp.float32),
             pltpu.VMEM((2, longest, LANES), jnp.float32),
             pltpu.VMEM((4, packed, SUBLANES, LANES), jnp.float32),
@@ -301,7 +306,9 @@
             pltpu.SemaphoreType.DMA((4,)),
             pltpu.SemaphoreType.DMA((halves,)),
         ],
-        compiler_params=pltpu.CompilerParams(collective_id=0, has_side_effects=True),
+        compiler_params=pltpu.CompilerParams(
+            collective_id=0, has_side_effects=True, vmem_limit_bytes=VMEM_BYTES
+        ),
     )(cost_volume.reshape(rows * cols, disparities), left_image, p_small, p_large)
     return total.reshape(rows, cols, disparities)
 

time: 33.2 us -> 30.1 us (0.907)
  Pallas kernels: 31.2 us -> 26.8 us
  local copies, waits for them, and re-layouts: 1.67 us -> 3.02 us
    pallas_call x1, Pallas kernels: 31.2 us -> 26.8 us  [on_device(): pl.pallas_call(functools.partial(kernel, rows, cols), out_shape=jax.Shape...]
    unnamed x1 -> x9, local copies, waits for them, and re-layouts: 1.67 us -> 3.02 us
where the time goes in v2:
time: 30.1 us; the launch traced here: 29.8 us
  Pallas kernels  26.8 us (89%)
  local copies, waits for them, and re-layouts  3.02 us (10%)
    pallas_call x1, Pallas kernels, on_device(): pl.pallas_call(functools.partial(kernel, rows, cols), out_shape=jax.Shape...  26.8 us
    unnamed x9, local copies, waits for them, and re-layouts  3.02 us

profile of v2, /device:TPU:0, one launch (start us, length us, event | category | flops | bytes accessed | tf_op | source)
XLA Modules:
  0.0 29.8 jit_solution(12513390369741774062)
XLA Ops:
  0.0 0.0 copy-start.3
  0.0 0.0 copy-start.2
  0.0 0.7 %copy-done.3 = s32[4]{0:T(128)S(1)} copy-done((s32[4]{0:T(128)S(1)}, s32[4]{0:T(128)}, u32[]{:S(2)}) %copy-start.3) | copy-done | bytes 40
  0.7 0.0 copy-done.2
  0.7 0.0 copy-start
  0.7 0.9 %copy-done = s32[16,16,256]{2,1,0:T(8,128)S(1)} copy-done((s32[16,16,256]{2,1,0:T(8,128)S(1)}, s32[16,16,256]{2,1,0:T(8,128)}, u32[]{:S(2)}) %copy-start) | copy-done | bytes 262168
  1.6 0.0 copy-start.1
  1.6 0.7 %copy-done.1 = f32[16,16]{1,0:T(8,128)S(1)} copy-done((f32[16,16]{1,0:T(8,128)S(1)}, f32[16,16]{1,0:T(8,128)}, u32[]{:S(2)}) %copy-start.1) | copy-done | bytes 1048
  2.3 26.8 %shard_map.46 = f32[256,256]{1,0:T(8,128)S(1)} custom-call(s32[256,256]{1,0:T(8,128)S(1)} %bitcast.3, f32[16,16]{1,0:T(8,128)S(1)} %copy-done.1, s32[4]{0:T(128)S(1)} %copy-done.2, s32[4]{0:T(128)S(1)} %copy-done.3), custom_call_target="tpu_custom_call" | custom-call | tf_op jit(solution)/shard_map/pallas_call | solution.py:286
  29.1 0.7 %copy.6 = f32[16,16,256]{2,1,0:T(8,128)} copy(f32[16,16,256]{2,1,0:T(8,128)S(1)} %bitcast.2) | data formatting | bytes 524288
Async XLA Ops:
  0.0 0.7 %copy-start.3 = (s32[4]{0:T(128)S(1)}, s32[4]{0:T(128)}, u32[]{:S(2)}) copy-start(s32[4]{0:T(128)} %large_ref.1) | copy-start | bytes 52
  0.0 0.7 %copy-start.2 = (s32[4]{0:T(128)S(1)}, s32[4]{0:T(128)}, u32[]{:S(2)}) copy-start(s32[4]{0:T(128)} %small_ref.1) | copy-start | bytes 52
  0.7 0.9 %copy-start = (s32[16,16,256]{2,1,0:T(8,128)S(1)}, s32[16,16,256]{2,1,0:T(8,128)}, u32[]{:S(2)}) copy-start(s32[16,16,256]{2,1,0:T(8,128)} %param.4) | copy-start | bytes 786436
  1.6 0.7 %copy-start.1 = (f32[16,16]{1,0:T(8,128)S(1)}, f32[16,16]{1,0:T(8,128)}, u32[]{:S(2)}) copy-start(f32[16,16]{1,0:T(8,128)} %image_ref.1) | copy-start | bytes 3076

commit v3 on v2

--- a/solution.py
+++ b/solution.py
@@ -36,15 +36,19 @@
     rows,
     cols,
     cost_ref,
+    image_hbm,
+    small_hbm,
+    large_hbm,
+    out_ref,
     image_ref,
     small_ref,
     large_ref,
-    out_ref,
     staged,
+    ordered,
+    order,
     totals,
     costs,
     paths,
-    turned,
     large_lines,
     image_lines,
     outbox,
@@ -80,8 +84,16 @@
             cost_ref.at[:, pl.ds(h * LANES, LANES)], staged.at[h], local_sems.at[h]
         )
 
+    small_copies = [
+        pltpu.make_async_copy(source, target, local_sems.at[halves + at])
+        for at, (source, target) in enumerate(
+            ((image_hbm, image_ref), (small_hbm, small_ref), (large_hbm, large_ref))
+        )
+    ]
     for h in range(halves):
         cost_copy(h).start()
+    for copy in small_copies:
+        copy.start()
 
     barrier = pltpu.get_barrier_semaphore()
     for k in range(4):
@@ -92,6 +104,14 @@
 
     neighbours = sum(jnp.where(flag, 1, 0) for flag in has_next)
 
+    shape = (disparities, disparities)
+    source = lax.broadcasted_iota(jnp.int32, shape, 0)
+    target = lax.broadcasted_iota(jnp.int32, shape, 1)
+    wanted = target // SUBLANES + nv * (target % SUBLANES)
+    order[...] = jnp.where(source == wanted, 1.0, 0.0).astype(jnp.bfloat16)
+
+    for copy in small_copies:
+        copy.wait()
     image = image_ref[...]
     image_lines[...] = jnp.zeros_like(image_lines)
     image_lines[0, :cols, :rows] = image.T
@@ -131,23 +151,28 @@
     for h in range(halves):
         cost_copy(h).wait()
 
-    def turn_in(slot, axis, line, at, count):
+    block = jnp.concatenate([staged[h] for h in range(halves)], axis=1)
+    block = block.astype(jnp.float32).astype(jnp.bfloat16)
+    block = jnp.dot(block, order[...], preferred_element_type=jnp.float32)
+    for h in range(halves):
+        ordered[h] = block[:, h * LANES : (h + 1) * LANES]
+
+    def turn_in(axis, line, at, count):
+        per = LANES // SUBLANES
         for h in range(halves):
-            block = staged[h, at, :].astype(jnp.float32)
-            turned[slot, h * LANES : (h + 1) * LANES, :count] = block.T
-        for v in range(nv):
-            costs[axis, line, v] = turned[slot, pl.ds(v, SUBLANES, stride=nv), :]
+            block = ordered[h, at, :].T.reshape(per, SUBLANES, count)
+            costs[axis, line, h * per : (h + 1) * per, :, :count] = block
 
     def turn_across(index, carry):
         for slot in range(BATCH):
             line = index * BATCH + slot
-            turn_in(slot, 0, line, pl.ds(line, rows, stride=cols), rows)
+            turn_in(0, line, pl.ds(line, rows, stride=cols), rows)
         return carry
 
     def turn_down(index, carry):
         for slot in range(BATCH):
             line = index * BATCH + slot
-            turn_in(slot, 1, line, pl.ds(pl.multiple_of(line * cols, cols), cols), cols)
+            turn_in(1, line, pl.ds(pl.multiple_of(line * cols, cols), cols), cols)
         return carry
 
     lax.fori_loop(0, cols // BATCH, turn_across, 0)
@@ -222,17 +247,20 @@
                 outbox[k, slot] = packed
             path_copy(k).start()
 
-    def turn_out(slot, k, line, count):
-        for v in range(nv):
-            total = paths[k, line, v] + paths[k + 1, line, v]
-            turned[slot, pl.ds(v, SUBLANES, stride=nv), :] = total
-        return [turned[slot, h * LANES : (h + 1) * LANES, :count].T for h in range(halves)]
+    def turn_out(k, line, count):
+        per = LANES // SUBLANES
+        parts = []
+        for h in range(halves):
+            at = pl.ds(h * per, per)
+            total = paths[k, line, at] + paths[k + 1, line, at]
+            parts.append(total.reshape(LANES, LANES)[:, :count].T)
+        return parts
 
     def down_total(index, carry):
         for slot in range(BATCH):
             line = index * BATCH + slot
             at = pl.ds(pl.multiple_of(line * cols, cols), cols)
-            for h, part in enumerate(turn_out(slot, 2, line, cols)):
+            for h, part in enumerate(turn_out(2, line, cols)):
                 totals[h, at, :] = part
         return carry
 
@@ -240,7 +268,7 @@
         for slot in range(BATCH):
             line = index * BATCH + slot
             at = pl.ds(line, rows, stride=cols)
-            for h, part in enumerate(turn_out(slot, 0, line, rows)):
+            for h, part in enumerate(turn_out(0, line, rows)):
                 totals[h, at, :] = totals[h, at, :] + part
         return carry
 
@@ -263,8 +291,17 @@
 
     lax.fori_loop(0, max(nx, ny + 4), one_turn, 0)
     lax.fori_loop(0, cols // BATCH, across_total, 0)
-    for h in range(halves):
-        out_ref[:, h * LANES : (h + 1) * LANES] = totals[h] * OUT_SCALE
+    rest = jnp.concatenate([totals[h] for h in range(halves)], axis=1) * OUT_SCALE
+    result = None
+    for part in range(3):
+        piece = rest.astype(jnp.bfloat16)
+        moved = lax.dot_general(
+            piece, order[...], (((1,), (1,)), ((), ())), preferred_element_type=jnp.float32
+        )
+        result = moved if part == 0 else result + moved
+        if part < 2:
+            rest = rest - piece.astype(jnp.float32)
+    out_ref[...] = result
 
     for k in range(4):
 
@@ -280,20 +317,23 @@
     longest = max(rows, cols)
     packed = nv * longest // LANES
     halves = disparities // LANES
-    hbm = pl.BlockSpec(memory_space=pl.ANY)
+    hbm = pl.BlockSpec(memory_space=pltpu.HBM)
     vmem = pl.BlockSpec(memory_space=pltpu.VMEM)
-    smem = pl.BlockSpec(memory_space=pltpu.SMEM)
     total = pl.pallas_call(
         functools.partial(kernel, rows, cols),
         out_shape=jax.ShapeDtypeStruct((rows * cols, disparities), jnp.float32),
-        in_specs=[hbm, vmem, smem, smem],
+        in_specs=[hbm] * 4,
         out_specs=vmem,
         scratch_shapes=[
+            pltpu.VMEM((rows, cols), jnp.float32),
+            pltpu.SMEM((4,), jnp.int32),
+            pltpu.SMEM((4,), jnp.int32),
             pltpu.VMEM((halves, rows * cols, LANES), jnp.int32),
+            pltpu.VMEM((halves, rows * cols, LANES), jnp.float32),
+            pltpu.VMEM((disparities, disparities), jnp.bfloat16),
             pltpu.VMEM((halves, rows * cols, LANES), jnp.float32),
             pltpu.VMEM((2, longest, nv, SUBLANES, LANES), jnp.float32),
             pltpu.VMEM((4, longest, nv, SUBLANES, LANES), jnp.float32),
-            pltpu.VMEM((BATCH, disparities, LANES), jnp.float32),
             pltpu.VMEM((4, longest, LANES), jnp.float32),
             pltpu.VMEM((2, longest, LANES), jnp.float32),
             pltpu.VMEM((4, packed, SUBLANES, LANES), jnp.float32),
@@ -304,7 +344,7 @@
             pltpu.SemaphoreType.DMA((4,)),
             pltpu.SemaphoreType.DMA((4,)),
             pltpu.SemaphoreType.DMA((4,)),
-            pltpu.SemaphoreType.DMA((halves,)),
+            pltpu.SemaphoreType.DMA((halves + 3,)),
         ],
         compiler_params=pltpu.CompilerParams(
             collective_id=0, has_side_effects=True, vmem_limit_bytes=VMEM_BYTES

time: 30.1 us -> 27.3 us (0.907)
  Pallas kernels: 26.8 us -> 24.1 us
    pallas_call x1, Pallas kernels: 26.8 us -> 24.1 us  [on_device(): pl.pallas_call(functools.partial(kernel, rows, cols), out_shape=jax.Shape...]
where the time goes in v3:
time: 27.3 us; the launch traced here: 27.1 us
  Pallas kernels  24.1 us (88%)
  local copies, waits for them, and re-layouts  3.02 us (11%)
    pallas_call x1, Pallas kernels, on_device(): pl.pallas_call(functools.partial(kernel, rows, cols), out_shape=jax.Shape...  24.1 us
    unnamed x9, local copies, waits for them, and re-layouts  3.02 us

profile of v3, /device:TPU:0, one launch (start us, length us, event | category | flops | bytes accessed | tf_op | source)
XLA Modules:
  0.0 27.1 jit_solution(8415120612848994374)
XLA Ops:
  0.0 0.0 copy-start.3
  0.0 0.0 copy-start.2
  0.0 0.7 %copy-done.3 = s32[4]{0:T(128)S(1)} copy-done((s32[4]{0:T(128)S(1)}, s32[4]{0:T(128)}, u32[]{:S(2)}) %copy-start.3) | copy-done | bytes 40
  0.7 0.0 copy-done.2
  0.7 0.0 copy-start
  0.7 0.9 %copy-done = s32[16,16,256]{2,1,0:T(8,128)S(1)} copy-done((s32[16,16,256]{2,1,0:T(8,128)S(1)}, s32[16,16,256]{2,1,0:T(8,128)}, u32[]{:S(2)}) %copy-start) | copy-done | bytes 262168
  1.6 0.0 copy-start.1
  1.6 0.7 %copy-done.1 = f32[16,16]{1,0:T(8,128)S(1)} copy-done((f32[16,16]{1,0:T(8,128)S(1)}, f32[16,16]{1,0:T(8,128)}, u32[]{:S(2)}) %copy-start.1) | copy-done | bytes 1048
  2.3 24.1 %shard_map.46 = f32[256,256]{1,0:T(8,128)S(1)} custom-call(s32[256,256]{1,0:T(8,128)S(1)} %bitcast.3, f32[16,16]{1,0:T(8,128)S(1)} %copy-done.1, s32[4]{0:T(128)S(1)} %copy-done.2, s32[4]{0:T(128)S(1)} %copy-done.3), custom_call_target="tpu_custom_call" | custom-call | tf_op jit(solution)/shard_map/pallas_call | solution.py:322
  26.4 0.7 %copy.6 = f32[16,16,256]{2,1,0:T(8,128)} copy(f32[16,16,256]{2,1,0:T(8,128)S(1)} %bitcast.2) | data formatting | bytes 524288
Async XLA Ops:
  0.0 0.7 %copy-start.3 = (s32[4]{0:T(128)S(1)}, s32[4]{0:T(128)}, u32[]{:S(2)}) copy-start(s32[4]{0:T(128)} %large_hbm.1) | copy-start | bytes 52
  0.0 0.7 %copy-start.2 = (s32[4]{0:T(128)S(1)}, s32[4]{0:T(128)}, u32[]{:S(2)}) copy-start(s32[4]{0:T(128)} %small_hbm.1) | copy-start | bytes 52
  0.7 0.9 %copy-start = (s32[16,16,256]{2,1,0:T(8,128)S(1)}, s32[16,16,256]{2,1,0:T(8,128)}, u32[]{:S(2)}) copy-start(s32[16,16,256]{2,1,0:T(8,128)} %param.4) | copy-start | bytes 786436
  1.6 0.7 %copy-start.1 = (f32[16,16]{1,0:T(8,128)S(1)}, f32[16,16]{1,0:T(8,128)}, u32[]{:S(2)}) copy-start(f32[16,16]{1,0:T(8,128)} %image_hbm.1) | copy-start | bytes 3076

commit v4 on v3

--- a/solution.py
+++ b/solution.py
@@ -120,7 +120,6 @@
     for k in range(4):
         last = 0 if backward[k] else lengths[k] - 1
         edge_out[k, 0:1, :] = image_lines[k // 2, last : last + 1, :]
-    pl.semaphore_wait(barrier, neighbours)
 
     def edge_copy(k):
         return pltpu.make_async_remote_copy(
@@ -142,12 +141,6 @@
             device_id_type=MESH,
         )
 
-    for k in range(4):
-
-        @pl.when(has_next[k])
-        def _(k=k):
-            edge_copy(k).start()
-
     for h in range(halves):
         cost_copy(h).wait()
 
@@ -176,6 +169,13 @@
         return carry
 
     lax.fori_loop(0, cols // BATCH, turn_across, 0)
+
+    pl.semaphore_wait(barrier, neighbours)
+    for k in range(4):
+
+        @pl.when(has_next[k])
+        def _(k=k):
+            edge_copy(k).start()
 
     sub = lax.broadcasted_iota(jnp.int32, (SUBLANES, LANES), 0)
     lane = lax.broadcasted_iota(jnp.int32, (SUBLANES, LANES), 1)
@@ -349,7 +349,17 @@
         compiler_params=pltpu.CompilerParams(
             collective_id=0, has_side_effects=True, vmem_limit_bytes=VMEM_BYTES
         ),
-    )(cost_volume.reshape(rows * cols, disparities), left_image, p_small, p_large)
+    )(
+        *(
+            pltpu.with_memory_space_constraint(array, pltpu.HBM)
+            for array in (
+                cost_volume.reshape(rows * cols, disparities),
+                left_image,
+                p_small,
+                p_large,
+            )
+        )
+    )
     return total.reshape(rows, cols, disparities)
 
 

time: 27.3 us -> 25.3 us (0.927)
  local copies, waits for them, and re-layouts: 3.02 us -> 0.71 us
  Pallas kernels: 24.1 us -> 24.4 us
    unnamed x9 -> x1, local copies, waits for them, and re-layouts: 3.02 us -> 0.71 us
    pallas_call x1, Pallas kernels: 24.1 us -> 24.4 us  [on_device(): pl.pallas_call(functools.partial(kernel, rows, cols), out_shape=jax.Shape...]
where the time goes in v4:
time: 25.3 us; the launch traced here: 25.1 us
  Pallas kernels  24.4 us (96%)
  local copies, waits for them, and re-layouts  0.71 us (3%)
    pallas_call x1, Pallas kernels, on_device(): pl.pallas_call(functools.partial(kernel, rows, cols), out_shape=jax.Shape...  24.4 us
    unnamed x1, local copies, waits for them, and re-layouts  0.71 us

profile of v4, /device:TPU:0, one launch (start us, length us, event | category | flops | bytes accessed | tf_op | source)
XLA Modules:
  0.0 25.1 jit_solution(17742830381441136353)
XLA Ops:
  0.0 24.4 %shard_map.46 = f32[256,256]{1,0:T(8,128)S(1)} custom-call(s32[256,256]{1,0:T(8,128)} %bitcast.3, f32[16,16]{1,0:T(8,128)} %image_hbm.1, s32[4]{0:T(128)} %small_hbm.1, s32[4]{0:T(128)} %large_hbm.1), custom_call_target="tpu_custom_call" | custom-call | tf_op jit(solution)/shard_map/pallas_call | solution.py:322
  24.4 0.7 %copy.6 = f32[16,16,256]{2,1,0:T(8,128)} copy(f32[16,16,256]{2,1,0:T(8,128)S(1)} %bitcast.2) | data formatting | bytes 524288

commit v5 on v4

--- a/solution.py
+++ b/solution.py
@@ -49,6 +49,7 @@
     totals,
     costs,
     paths,
+    lowests,
     large_lines,
     image_lines,
     outbox,
@@ -180,7 +181,14 @@
     sub = lax.broadcasted_iota(jnp.int32, (SUBLANES, LANES), 0)
     lane = lax.broadcasted_iota(jnp.int32, (SUBLANES, LANES), 1)
 
-    def task(k):
+    def turn_back(registers, count):
+        per = LANES // SUBLANES
+        return [
+            jnp.concatenate(registers[h * per : (h + 1) * per], axis=0)[:, :count].T
+            for h in range(halves)
+        ]
+
+    def task(k, last=False):
         axis = k // 2
         length, width = lengths[k], lines[k]
         group = LANES // width
@@ -218,6 +226,7 @@
             line = length - 1 - index if backward[k] else index
             capped = large_lines[k, pl.ds(line, SUBLANES, stride=0), :]
             lowest = all_sublanes_min(tree_min(state))
+            capped = capped + lowest
             under = jnp.where(sub == 0, FAR, pltpu.roll(state[-1], 1, 0))
             over = jnp.where(sub == SUBLANES - 1, FAR, pltpu.roll(state[0], SUBLANES - 1, 0))
             fresh = []
@@ -225,9 +234,17 @@
                 low = state[v - 1] if v else under
                 high = state[v + 1] if v < nv - 1 else over
                 near = jnp.minimum(state[v], jnp.minimum(low, high) + small)
-                value = costs[axis, line, v] + jnp.minimum(near - lowest, capped)
-                paths[k, line, v] = value
-                fresh.append(value)
+                fresh.append(costs[axis, line, v] + jnp.minimum(near, capped))
+            if last:
+                above = lowest + lowests[k ^ 1, line]
+                both = [fresh[v] + paths[k ^ 1, line, v] - above for v in range(nv)]
+                at = pl.ds(line, rows, stride=cols)
+                for h, part in enumerate(turn_back(both, rows)):
+                    totals[0, h, at, :] = part
+            else:
+                for v in range(nv):
+                    paths[k, line, v] = fresh[v]
+            lowests[k, line] = lowest
             return tuple(fresh)
 
         def steps(index, state):
@@ -239,46 +256,38 @@
 
         @pl.when(has_next[k])
         def _():
+            above = lowests[k, 0 if backward[k] else length - 1]
+            sent = [part - above for part in state]
             for slot in range(nv // group):
-                packed = state[slot * group]
+                packed = sent[slot * group]
                 for g in range(1, group):
-                    moved = pltpu.roll(state[slot * group + g], g * width, 1)
+                    moved = pltpu.roll(sent[slot * group + g], g * width, 1)
                     packed = jnp.where(lane >= g * width, moved, packed)
                 outbox[k, slot] = packed
             path_copy(k).start()
-
-    def turn_out(k, line, count):
-        per = LANES // SUBLANES
-        parts = []
-        for h in range(halves):
-            at = pl.ds(h * per, per)
-            total = paths[k, line, at] + paths[k + 1, line, at]
-            parts.append(total.reshape(LANES, LANES)[:, :count].T)
-        return parts
 
     def down_total(index, carry):
         for slot in range(BATCH):
             line = index * BATCH + slot
             at = pl.ds(pl.multiple_of(line * cols, cols), cols)
-            for h, part in enumerate(turn_out(2, line, cols)):
-                totals[h, at, :] = part
+            above = lowests[2, line] + lowests[3, line]
+            both = [paths[2, line, v] + paths[3, line, v] - above for v in range(nv)]
+            for h, part in enumerate(turn_back(both, cols)):
+                totals[1, h, at, :] = part
         return carry
 
-    def across_total(index, carry):
-        for slot in range(BATCH):
-            line = index * BATCH + slot
-            at = pl.ds(line, rows, stride=cols)
-            for h, part in enumerate(turn_out(0, line, rows)):
-                totals[h, at, :] = totals[h, at, :] + part
-        return carry
-
+    right_first = ix <= nx - 1 - ix
+    left_first = ix > nx - 1 - ix
     low_turn = jnp.minimum(ix, nx - 1 - ix)
     high_turn = jnp.maximum(ix, nx - 1 - ix)
     spare = jnp.where(low_turn >= 3, low_turn - 1, 2 * nx + 2 * ny)
 
     def one_turn(turn, carry):
-        pl.when(turn == ix)(lambda: task(0))
-        pl.when(turn == nx - 1 - ix)(lambda: task(1))
+        right_turn, left_turn = turn == ix, turn == nx - 1 - ix
+        pl.when(jnp.logical_and(right_turn, right_first))(lambda: task(0))
+        pl.when(jnp.logical_and(left_turn, left_first))(lambda: task(1))
+        pl.when(jnp.logical_and(right_turn, left_first))(lambda: task(0, last=True))
+        pl.when(jnp.logical_and(left_turn, right_first))(lambda: task(1, last=True))
         taken = jnp.logical_or(turn == low_turn, turn == high_turn)
         taken = jnp.logical_or(taken, turn == spare)
         used = sum(jnp.where(at < turn, 1, 0) for at in (low_turn, high_turn, spare))
@@ -290,8 +299,8 @@
         return carry
 
     lax.fori_loop(0, max(nx, ny + 4), one_turn, 0)
-    lax.fori_loop(0, cols // BATCH, across_total, 0)
-    rest = jnp.concatenate([totals[h] for h in range(halves)], axis=1) * OUT_SCALE
+    rest = jnp.concatenate([totals[0, h] + totals[1, h] for h in range(halves)], axis=1)
+    rest = rest * OUT_SCALE
     result = None
     for part in range(3):
         piece = rest.astype(jnp.bfloat16)
@@ -331,9 +340,10 @@
             pltpu.VMEM((halves, rows * cols, LANES), jnp.int32),
             pltpu.VMEM((halves, rows * cols, LANES), jnp.float32),
             pltpu.VMEM((disparities, disparities), jnp.bfloat16),
-            pltpu.VMEM((halves, rows * cols, LANES), jnp.float32),
+            pltpu.VMEM((2, halves, rows * cols, LANES), jnp.float32),
             pltpu.VMEM((2, longest, nv, SUBLANES, LANES), jnp.float32),
             pltpu.VMEM((4, longest, nv, SUBLANES, LANES), jnp.float32),
+            pltpu.VMEM((4, longest, SUBLANES, LANES), jnp.float32),
             pltpu.VMEM((4, longest, LANES), jnp.float32),
             pltpu.VMEM((2, longest, LANES), jnp.float32),
             pltpu.VMEM((4, packed, SUBLANES, LANES), jnp.float32),

time: 25.3 us -> 26.1 us (1.032)
  Pallas kernels: 24.4 us -> 25.3 us
    pallas_call x1, Pallas kernels: 24.4 us -> 25.3 us  [on_device(): pl.pallas_call(functools.partial(kernel, rows, cols), out_shape=jax.Shape...]
where the time goes in v5:
time: 26.1 us; the launch traced here: 26 us
  Pallas kernels  25.3 us (97%)
  local copies, waits for them, and re-layouts  0.71 us (3%)
    pallas_call x1, Pallas kernels, on_device(): pl.pallas_call(functools.partial(kernel, rows, cols), out_shape=jax.Shape...  25.3 us
    unnamed x1, local copies, waits for them, and re-layouts  0.71 us

profile of v5, /device:TPU:0, one launch (start us, length us, event | category | flops | bytes accessed | tf_op | source)
XLA Modules:
  0.0 26.0 jit_solution(16575235476648192508)
XLA Ops:
  0.0 25.3 %shard_map.46 = f32[256,256]{1,0:T(8,128)S(1)} custom-call(s32[256,256]{1,0:T(8,128)} %bitcast.3, f32[16,16]{1,0:T(8,128)} %image_hbm.1, s32[4]{0:T(128)} %small_hbm.1, s32[4]{0:T(128)} %large_hbm.1), custom_call_target="tpu_custom_call" | custom-call | tf_op jit(solution)/shard_map/pallas_call | solution.py:331
  25.3 0.7 %copy.6 = f32[16,16,256]{2,1,0:T(8,128)} copy(f32[16,16,256]{2,1,0:T(8,128)S(1)} %bitcast.2) | data formatting | bytes 524288

commit v6 on v5

--- a/solution.py
+++ b/solution.py
@@ -188,7 +188,7 @@
             for h in range(halves)
         ]
 
-    def task(k, last=False):
+    def task(k):
         axis = k // 2
         length, width = lengths[k], lines[k]
         group = LANES // width
@@ -235,15 +235,8 @@
                 high = state[v + 1] if v < nv - 1 else over
                 near = jnp.minimum(state[v], jnp.minimum(low, high) + small)
                 fresh.append(costs[axis, line, v] + jnp.minimum(near, capped))
-            if last:
-                above = lowest + lowests[k ^ 1, line]
-                both = [fresh[v] + paths[k ^ 1, line, v] - above for v in range(nv)]
-                at = pl.ds(line, rows, stride=cols)
-                for h, part in enumerate(turn_back(both, rows)):
-                    totals[0, h, at, :] = part
-            else:
-                for v in range(nv):
-                    paths[k, line, v] = fresh[v]
+            for v in range(nv):
+                paths[k, line, v] = fresh[v]
             lowests[k, line] = lowest
             return tuple(fresh)
 
@@ -266,28 +259,35 @@
                 outbox[k, slot] = packed
             path_copy(k).start()
 
+    def both_ways(k, line, count):
+        above = lowests[k, line] + lowests[k + 1, line]
+        return turn_back(
+            [paths[k, line, v] + paths[k + 1, line, v] - above for v in range(nv)], count
+        )
+
     def down_total(index, carry):
         for slot in range(BATCH):
             line = index * BATCH + slot
             at = pl.ds(pl.multiple_of(line * cols, cols), cols)
-            above = lowests[2, line] + lowests[3, line]
-            both = [paths[2, line, v] + paths[3, line, v] - above for v in range(nv)]
-            for h, part in enumerate(turn_back(both, cols)):
+            for h, part in enumerate(both_ways(2, line, cols)):
                 totals[1, h, at, :] = part
         return carry
 
-    right_first = ix <= nx - 1 - ix
-    left_first = ix > nx - 1 - ix
+    def across_total(index, carry):
+        for slot in range(BATCH):
+            line = index * BATCH + slot
+            at = pl.ds(line, rows, stride=cols)
+            for h, part in enumerate(both_ways(0, line, rows)):
+                totals[0, h, at, :] = part
+        return carry
+
     low_turn = jnp.minimum(ix, nx - 1 - ix)
     high_turn = jnp.maximum(ix, nx - 1 - ix)
     spare = jnp.where(low_turn >= 3, low_turn - 1, 2 * nx + 2 * ny)
 
     def one_turn(turn, carry):
-        right_turn, left_turn = turn == ix, turn == nx - 1 - ix
-        pl.when(jnp.logical_and(right_turn, right_first))(lambda: task(0))
-        pl.when(jnp.logical_and(left_turn, left_first))(lambda: task(1))
-        pl.when(jnp.logical_and(right_turn, left_first))(lambda: task(0, last=True))
-        pl.when(jnp.logical_and(left_turn, right_first))(lambda: task(1, last=True))
+        pl.when(turn == ix)(lambda: task(0))
+        pl.when(turn == nx - 1 - ix)(lambda: task(1))
         taken = jnp.logical_or(turn == low_turn, turn == high_turn)
         taken = jnp.logical_or(taken, turn == spare)
         used = sum(jnp.where(at < turn, 1, 0) for at in (low_turn, high_turn, spare))
@@ -299,6 +299,7 @@
         return carry
 
     lax.fori_loop(0, max(nx, ny + 4), one_turn, 0)
+    lax.fori_loop(0, cols // BATCH, across_total, 0)
     rest = jnp.concatenate([totals[0, h] + totals[1, h] for h in range(halves)], axis=1)
     rest = rest * OUT_SCALE
     result = None

time: 26.1 us -> 25 us (0.958)
  Pallas kernels: 25.3 us -> 24.2 us
    pallas_call x1, Pallas kernels: 25.3 us -> 24.2 us  [on_device(): pl.pallas_call(functools.partial(kernel, rows, cols), out_shape=jax.Shape...]
where the time goes in v6:
time: 25 us; the launch traced here: 24.9 us
  Pallas kernels  24.2 us (97%)
  local copies, waits for them, and re-layouts  0.71 us (3%)
    pallas_call x1, Pallas kernels, on_device(): pl.pallas_call(functools.partial(kernel, rows, cols), out_shape=jax.Shape...  24.2 us
    unnamed x1, local copies, waits for them, and re-layouts  0.71 us

profile of v6, /device:TPU:0, one launch (start us, length us, event | category | flops | bytes accessed | tf_op | source)
XLA Modules:
  0.0 24.9 jit_solution(11988005964498058366)
XLA Ops:
  0.0 24.2 %shard_map.46 = f32[256,256]{1,0:T(8,128)S(1)} custom-call(s32[256,256]{1,0:T(8,128)} %bitcast.3, f32[16,16]{1,0:T(8,128)} %image_hbm.1, s32[4]{0:T(128)} %small_hbm.1, s32[4]{0:T(128)} %large_hbm.1), custom_call_target="tpu_custom_call" | custom-call | tf_op jit(solution)/shard_map/pallas_call | solution.py:332
  24.2 0.7 %copy.6 = f32[16,16,256]{2,1,0:T(8,128)} copy(f32[16,16,256]{2,1,0:T(8,128)S(1)} %bitcast.2) | data formatting | bytes 524288
